TPU v7x, 32 devices: a whole 2x2x4 slice. The times are simulated.
32 devices in a mesh: dp: 2 (over y), table: 16 (over z, x, core).
Axes of the slice: x: 2, y: 2, z: 4, core: 2. Of those that a mesh axis runs over, the one named last changes fastest.
Arguments:
- gradients: bfloat16 [256, 4096], P(None, ('dp', 'table')), may hold values from -16 to 16
- row_ids: int32 [4096], P(('dp', 'table')), may hold values from 0 to 32767
- table_block: float32 [256, 32768], P('table', 'dp'), may hold values from -6 to 6
- adagrad_state: float32 [32768], P('dp'), may hold values from 0.05 to 2
Outputs:
- new_table: float32 [256, 32768], P('table', 'dp')
- new_state: float32 [32768], P('dp')
All inputs are finite; a program needn't handle non-finite values.
Results may differ from a plain program's by a relative error of at most 0.0003.
Values may be sent and summed in bfloat16 or wider, within the bound.
A program may use at most 64 MiB of HBM per device.

v0:
```python
import jax
import jax.numpy as jnp
from jax import lax
from jax.sharding import PartitionSpec as P

W = 256


learn_rate = 0.5


def accumulate(grads, ids, first_row, count_rows):
    relative = ids - first_row
    inside = (relative >= 0) & (relative < count_rows)
    target = jnp.where(inside, relative, count_rows)
    start_total = jnp.zeros((grads.shape[0], count_rows), jnp.float32)
    return start_total.at[:, target].add(grads.astype(jnp.float32), mode="drop")


def body(gradients, row_ids, table_block, adagrad_state):
    owned = lax.all_to_all(gradients, "table", split_axis=0, concat_axis=1, tiled=True)
    local_rows = table_block.shape[1]
    all_row_ids = lax.all_gather(row_ids, ("dp", "table"), axis=0, tiled=True)
    first_row = lax.axis_index("dp") * local_rows
    row_grad = accumulate(
        lax.all_gather(owned, "dp", axis=1, tiled=True), all_row_ids, first_row, local_rows
    )
    partial_squares = jnp.sum(row_grad * row_grad, axis=0)
    squares = lax.psum(partial_squares, "table")
    new_state = adagrad_state + squares / W
    new_table = table_block - learn_rate * row_grad / jnp.sqrt(new_state)[None, :]
    return (new_table, new_state)


def solution(mesh):
    in_specs = (P(None, ("dp", "table")), P(("dp", "table")), P("table", "dp"), P("dp"))
    out_specs = (P("table", "dp"), P("dp"))
    return jax.shard_map(body, mesh=mesh, in_specs=in_specs, out_specs=out_specs, check_vma=False)
```

profile of v0, /device:TPU:0, one launch (start us, length us, event | category | flops | bytes accessed | tf_op | source)
XLA Modules:
  0.0 213.6 jit_solution(18062439507933522561)
XLA Ops:
  7.2 7.4 %all-to-all-start = ((bf16[16,16,128]{2,1,0:T(8,128)(2,1)}), bf16[16,16,128]{2,1,0:T(8,128)(2,1)S(1)}, u32[]{:S(2)}, u32[]{:S(2)}) async-start(bf16[16,16,128]{2,1,0:T(8,128)(2,1)} %bitcast.12), calls=%async_computation | async-start | bytes 131072 | tf_op jit(solution)/shard_map/all_to_all | solution.py:21
  14.6 0.0 all-reduce.2.cloned.1.call-start
  14.6 42.1 %all-gather = s32[32,1,128]{2,1,0:T(1,128)S(1)} all-gather(s32[1,1,128]{2,1,0:T(1,128)} %bitcast.15), channel_id=1, replica_groups=mesh['dp'=2,'table'=16] {'dp','table'}, dimensions={0}, use_global_device_ids=true | all-gather | bytes 16896 | tf_op jit(solution)/shard_map/all_gather | solution.py:23
  56.7 0.0 all-to-all-done
  56.7 0.3 copy.9
  57.0 14.8 %all_gather.7 = bf16[16,4096]{0,1:T(8,128)(2,1)S(1)} all-gather(bf16[16,2048]{0,1:T(8,128)(2,1)S(1)} %bitcast.10), channel_id=1, replica_groups=mesh['dp'=2,'table'=16] {'dp'}, dimensions={1}, use_global_device_ids=true | all-gather | bytes 196608 | tf_op jit(solution)/shard_map/all_gather | solution.py:26
  71.9 0.0 copy-start
  71.9 26.1 %scatter_custom_fusion = f32[16,16384]{0,1:T(8,128)} fusion(s32[4096]{0:T(1024)S(1)} %compare_select_fusion, f32[]{:T(128)} %constant.7.clone.1, bf16[16,4096]{0,1:T(8,128)(2,1)S(1)} %all_gather.7), kind=kCustom, calls=%fused_computation.3 | custom fusion | flops 131072 | bytes 2097156 | tf_op jit(solution)/shard_map/scatter-add | solution.py:17
  98.0 0.0 copy-start.1
  98.0 5.3 %multiply_reduce_fusion = f32[16384]{0:T(1024)} fusion(f32[16,16384]{0,1:T(8,128)} %scatter_custom_fusion), kind=kLoop, calls=%fused_computation.2 | loop fusion | flops 507904 | bytes 1114112 | tf_op jit(solution)/shard_map/reduce_sum | solution.py:28
  103.3 0.0 all-reduce.2.cloned.1.call-update
  103.3 0.0 copy-done
  103.3 4.6 %copy.10 = f32[16,16384]{0,1:T(8,128)} copy(f32[16,16384]{1,0:T(8,128)S(1)} %copy-done) | data formatting | bytes 2097152 | tf_op args[2]
  107.9 78.1 %all-reduce.2.cloned.1.call-done = f32[16384]{0:T(1024)} async-done(((f32[16384]{0:T(1024)}), f32[16384]{0:T(1024)}) %all-reduce.2.cloned.1.call-update) | async-done | bytes 65552 | tf_op jit(solution)/shard_map/psum | solution.py:29
  186.0 0.0 copy-done.1
  186.0 1.5 fusion.4
  187.5 13.3 %divide_subtract_fusion = f32[16,16384]{0,1:T(8,128)} fusion(f32[16,16384]{0,1:T(8,128)} %copy.10, f32[16,16384]{0,1:T(8,128)} %scatter_custom_fusion, f32[16384]{0:T(1024)S(1)} %get-tuple-element.6), kind=kLoop, calls=%fused_computation.1 | loop fusion | flops 786432 | bytes 3211264 | tf_op jit(solution)/shard_map/sub | solution.py:31
  200.8 6.0 %copy.11 = f32[16,16384]{1,0:T(8,128)} copy(f32[16,16384]{0,1:T(8,128)} %divide_subtract_fusion) | data formatting | bytes 2097152
  (2 shorter events, 0.0 us)
Async XLA Ops:
  7.2 49.6 %all-to-all-start = ((bf16[16,16,128]{2,1,0:T(8,128)(2,1)}), bf16[16,16,128]{2,1,0:T(8,128)(2,1)S(1)}, u32[]{:S(2)}, u32[]{:S(2)}) async-start(bf16[16,16,128]{2,1,0:T(8,128)(2,1)} %bitcast.12), calls=%async_computation | async-start | bytes 131072 | tf_op jit(solution)/shard_map/all_to_all | solution.py:21
  14.6 171.4 %all-reduce.2.cloned.1.call-start = ((), (), s32[]{:S(2)}) async-start(), calls=%async_computation.1 | async-start | bytes 131072 | tf_op jit(solution)/shard_map/psum | solution.py:29
  71.9 31.4 %copy-start = (f32[16,16384]{1,0:T(8,128)S(1)}, f32[16,16384]{1,0:T(8,128)}, u32[]{:S(2)}) copy-start(f32[16,16384]{1,0:T(8,128)} %param.6) | copy-start | bytes 3145732
  98.0 88.0 %copy-start.1 = (f32[16384]{0:T(1024)S(1)}, f32[16384]{0:T(1024)}, u32[]{:S(2)}) copy-start(f32[16384]{0:T(1024)} %param.7) | copy-start | bytes 196612
Sparse Core Ops, SparseCore 0:
  103.4 82.5 all-reduce.1
where the time goes:
time: 215 us; the launch traced here: 214 us
  waiting for transfers between devices  78.1 us (36%)
  blocking collectives  56.9 us (26%)
  other arithmetic  46.2 us (21%)
  between operations  14.1 us (7%)
  local copies, waits for them, and re-layouts  10.9 us (5%)
  starting transfers between devices  7.44 us (3%)
    psum x1, waiting for transfers between devices, body(): squares = lax.psum(partial_squares, 'table')  78.1 us
    all_gather x1, blocking collectives, body(): all_row_ids = lax.all_gather(row_ids, ('dp', 'table'), axis=0, tiled=True)  42.1 us
    scatter-add x1, other arithmetic, accumulate(): return start_total.at[:, target].add(grads.astype(jnp.float32), mode='drop')  26.1 us
    all_gather x1, blocking collectives, body(): lax.all_gather(owned, 'dp', axis=1, tiled=True)  14.8 us
    sub x1, other arithmetic, body(): table_block - learn_rate * row_grad / jnp.sqrt(new_state)[None, :]  13.3 us
    unnamed x6, local copies, waits for them, and re-layouts  10.6 us
    all_to_all x1, starting transfers between devices, body(): lax.all_to_all(gradients, 'table', split_axis=0, concat_axis=1, tiled=True)  7.4 us
    reduce_sum x1, other arithmetic, body(): partial_squares = jnp.sum(row_grad * row_grad, axis=0)  5.28 us
  transfers between devices with their start and end apart: 2, of which 1 were waited for; matrix products, arithmetic and copies ran while one was open for 2% of the time, Pallas kernels for 0%

commit v1 on v0

v1 whole, which is shorter than its diff:
```python
import functools

import jax
import jax.numpy as jnp
from jax import lax
from jax.experimental import pallas as pl
from jax.experimental.pallas import tpu as pltpu
from jax.sharding import PartitionSpec as P

learn_rate = 0.5
LO = 256
LANES = 128
MESH = pl.DeviceIdType.MESH


def accumulate(grads, ids, first_row, count_rows):
    relative = ids - first_row
    inside = (relative >= 0) & (relative < count_rows)
    target = jnp.where(inside, relative, count_rows)
    start_total = jnp.zeros((grads.shape[0], count_rows), jnp.float32)
    return start_total.at[:, target].add(grads.astype(jnp.float32), mode="drop")


def plain_body(width, gradients, row_ids, table_block, adagrad_state):
    owned = lax.all_to_all(gradients, "table", split_axis=0, concat_axis=1, tiled=True)
    local_rows = table_block.shape[1]
    all_row_ids = lax.all_gather(row_ids, ("dp", "table"), axis=0, tiled=True)
    first_row = lax.axis_index("dp") * local_rows
    row_grad = accumulate(
        lax.all_gather(owned, "dp", axis=1, tiled=True), all_row_ids, first_row, local_rows
    )
    partial_squares = jnp.sum(row_grad * row_grad, axis=0)
    squares = lax.psum(partial_squares, "table")
    new_state = adagrad_state + squares / width
    new_table = table_block - learn_rate * row_grad / jnp.sqrt(new_state)[None, :]
    return (new_table, new_state)


def exchange_kernel(
    dp, tb, cols, rows,
    g_ref, id_ref, acc_out, sq_ref,
    acc, got_g, got_i, part, red, total, full,
    send_g, send_i, send_r, send_a, recv_g, recv_i, recv_r, recv_a, own_sem, acc_sem,
):
    d, t = lax.axis_index("dp"), lax.axis_index("table")
    n = dp * tb
    me = d * tb + t
    his = rows // LO
    first_row = d * rows

    barrier = pltpu.get_barrier_semaphore()

    @pl.loop(1, n)
    def _(k):
        peer = lax.rem(me + k, n)
        pl.semaphore_signal(
            barrier, inc=1, device_id=(peer // tb, lax.rem(peer, tb)), device_id_type=MESH
        )

    own_g = pltpu.make_async_copy(g_ref.at[t], got_g.at[me], own_sem.at[0])
    own_i = pltpu.make_async_copy(id_ref, got_i.at[me], own_sem.at[1])
    own_g.start()
    own_i.start()
    acc[...] = jnp.zeros_like(acc)
    pl.semaphore_wait(barrier, n - 1)

    def block_copies(k):
        peer = lax.rem(me + k, n)
        to = (peer // tb, lax.rem(peer, tb))
        return (
            pltpu.make_async_remote_copy(
                src_ref=id_ref, dst_ref=got_i.at[me],
                send_sem=send_i.at[peer], recv_sem=recv_i.at[me],
                device_id=to, device_id_type=MESH,
            ),
            pltpu.make_async_remote_copy(
                src_ref=g_ref.at[to[1]], dst_ref=got_g.at[me],
                send_sem=send_g.at[peer], recv_sem=recv_g.at[me],
                device_id=to, device_id_type=MESH,
            ),
        )

    @pl.loop(1, n)
    def _(k):
        for copy in block_copies(k):
            copy.start()

    own_g.wait()
    own_i.wait()

    @pl.loop(1, n)
    def _(k):
        source = lax.rem(me + k, n)
        pltpu.make_async_copy(id_ref, got_i.at[source], recv_i.at[source]).wait()
        pltpu.make_async_copy(g_ref.at[t], got_g.at[source], recv_g.at[source]).wait()

    @pl.loop(0, n // 2)
    def _(k):
        ids = jnp.concatenate([got_i[2 * k], got_i[2 * k + 1]], axis=1) - first_row
        grads = jnp.concatenate([got_g[2 * k], got_g[2 * k + 1]], axis=1)
        span = ids.shape[1]
        low = jnp.broadcast_to(lax.bitwise_and(ids, LO - 1), (LO, span))
        place = lax.broadcasted_iota(jnp.int32, (LO, span), 0)
        one_hot = jnp.where(low == place, 1.0, 0.0).astype(jnp.bfloat16)
        high = jnp.broadcast_to(lax.shift_right_arithmetic(ids, 8), (cols, span))
        wide = grads.astype(jnp.float32)
        picked = jnp.concatenate(
            [jnp.where(high == h, wide, 0.0).astype(jnp.bfloat16) for h in range(his)], axis=0
        )
        acc[...] += lax.dot_general(
            picked, one_hot, (((1,), (1,)), ((), ())), preferred_element_type=jnp.float32
        )

    out_copy = pltpu.make_async_copy(acc, acc_out, acc_sem)
    out_copy.start()

    each = his // tb

    @pl.loop(0, tb)
    def _(j):
        lines = []
        for h in range(each):
            at = pl.multiple_of((j * each + h) * cols, cols)
            piece = acc[pl.ds(at, cols), :]
            sums = jnp.sum(piece * piece, axis=0, keepdims=True)
            for half in range(LO // LANES):
                lines.append(sums[:, half * LANES:(half + 1) * LANES])
        part[j] = jnp.concatenate(lines, axis=0)

    @pl.loop(1, tb)
    def _(k):
        to = lax.rem(t + k, tb)
        pltpu.make_async_remote_copy(
            src_ref=part.at[to], dst_ref=red.at[t],
            send_sem=send_r.at[to], recv_sem=recv_r.at[t],
            device_id=(d, to), device_id_type=MESH,
        ).start()

    @pl.loop(1, tb)
    def _(k):
        source = lax.rem(t + k, tb)
        pltpu.make_async_copy(part.at[t], red.at[source], recv_r.at[source]).wait()

    red[t] = part[t]
    total[...] = jnp.sum(red[...], axis=0)
    full[t] = total[...]

    @pl.loop(1, tb)
    def _(k):
        to = lax.rem(t + k, tb)
        pltpu.make_async_remote_copy(
            src_ref=total, dst_ref=full.at[t],
            send_sem=send_a.at[to], recv_sem=recv_a.at[t],
            device_id=(d, to), device_id_type=MESH,
        ).start()

    @pl.loop(1, n)
    def _(k):
        for copy in block_copies(k):
            copy.wait_send()

    @pl.loop(1, tb)
    def _(k):
        to = lax.rem(t + k, tb)
        pltpu.make_async_copy(part.at[to], red.at[t], send_r.at[to]).wait()
        pltpu.make_async_copy(total, full.at[t], send_a.at[to]).wait()

    @pl.loop(1, tb)
    def _(k):
        source = lax.rem(t + k, tb)
        pltpu.make_async_copy(total, full.at[source], recv_a.at[source]).wait()

    sq_ref[...] = full[...]
    out_copy.wait()


def update_kernel(width, cols, acc_ref, sq_ref, state_ref, table_ref, table_out, state_out):
    state = state_ref[...] + sq_ref[...] / width
    state_out[...] = state
    scale = learn_rate / jnp.sqrt(state)
    parts = LO // LANES
    for r in range(scale.shape[0]):
        h, half = r // parts, r % parts
        lanes = slice(r * LANES, (r + 1) * LANES)
        step = acc_ref[h * cols:(h + 1) * cols, half * LANES:(half + 1) * LANES]
        table_out[:, lanes] = table_ref[:, lanes] - step * scale[r:r + 1, :]


def kernel_body(dp, tb, width, gradients, row_ids, table_block, adagrad_state):
    cols, rows = table_block.shape
    count = row_ids.shape[0]
    n = dp * tb
    his = rows // LO
    lines = rows // tb // LANES
    dma = pltpu.SemaphoreType.DMA
    acc, squares = pl.pallas_call(
        functools.partial(exchange_kernel, dp, tb, cols, rows),
        name="exchange",
        out_shape=(
            jax.ShapeDtypeStruct((his * cols, LO), jnp.float32),
            jax.ShapeDtypeStruct((tb, lines, LANES), jnp.float32),
        ),
        in_specs=[pl.BlockSpec(memory_space=pl.ANY)] * 2,
        out_specs=(
            pl.BlockSpec(memory_space=pl.ANY),
            pl.BlockSpec(memory_space=pltpu.VMEM),
        ),
        scratch_shapes=[
            pltpu.VMEM((his * cols, LO), jnp.float32),
            pltpu.VMEM((n, cols, count), jnp.bfloat16),
            pltpu.VMEM((n, 1, count), jnp.int32),
            pltpu.VMEM((tb, lines, LANES), jnp.float32),
            pltpu.VMEM((tb, lines, LANES), jnp.float32),
            pltpu.VMEM((lines, LANES), jnp.float32),
            pltpu.VMEM((tb, lines, LANES), jnp.float32),
            dma((n,)), dma((n,)), dma((tb,)), dma((tb,)),
            dma((n,)), dma((n,)), dma((tb,)), dma((tb,)),
            dma((2,)), dma,
        ],
        compiler_params=pltpu.CompilerParams(collective_id=0, has_side_effects=True),
    )(gradients.reshape(tb, cols, count), row_ids.reshape(1, count))

    steps = 4
    block = rows // steps
    flat = (rows // LANES, LANES)
    line_spec = pl.BlockSpec((block // LANES, LANES), lambda i: (i, 0))
    wide_spec = pl.BlockSpec((cols, block), lambda i: (0, i))
    new_table, new_state = pl.pallas_call(
        functools.partial(update_kernel, width, cols),
        name="update",
        grid=(steps,),
        out_shape=(
            jax.ShapeDtypeStruct((cols, rows), jnp.float32),
            jax.ShapeDtypeStruct(flat, jnp.float32),
        ),
        in_specs=[
            pl.BlockSpec((his * cols // steps, LO), lambda i: (i, 0)),
            line_spec, line_spec, wide_spec,
        ],
        out_specs=(wide_spec, line_spec),
    )(acc, squares.reshape(flat), adagrad_state.reshape(flat), table_block)
    return (new_table, new_state.reshape(rows))


def body(dp, tb, gradients, row_ids, table_block, adagrad_state):
    width = gradients.shape[0]
    cols, rows = table_block.shape
    fits = (
        cols % 16 == 0
        and rows % (tb * 8 * LANES) == 0
        and rows % (4 * LO * 4) == 0
        and (dp * tb) % 2 == 0
        and row_ids.shape[0] == LANES
    )
    args = (gradients, row_ids, table_block, adagrad_state)
    if fits:
        return kernel_body(dp, tb, width, *args)
    return plain_body(width, *args)


def solution(mesh):
    in_specs = (P(None, ("dp", "table")), P(("dp", "table")), P("table", "dp"), P("dp"))
    out_specs = (P("table", "dp"), P("dp"))
    run = functools.partial(body, mesh.shape["dp"], mesh.shape["table"])
    return jax.shard_map(run, mesh=mesh, in_specs=in_specs, out_specs=out_specs, check_vma=False)
```

time: 215 us -> 33.1 us (0.15)
  waiting for transfers between devices: 78.1 us -> 0 us
  blocking collectives: 56.9 us -> 0 us
  other arithmetic: 46.2 us -> 0 us
  Pallas kernels: 0 us -> 32.3 us
  between operations: 14.1 us -> 0.64 us
  local copies, waits for them, and re-layouts: 10.9 us -> 0 us
  starting transfers between devices: 7.44 us -> 0 us
    psum x1 -> x0, waiting for transfers between devices: 78.1 us -> none  [body(): squares = lax.psum(partial_squares, 'table')]
    all_gather x2 -> x0, blocking collectives: 56.9 us -> none  [the longest x1 42.1 us: body(): all_row_ids = lax.all_gather(row_ids, ('dp', 'table'), axis=0, tiled=True)]
    pallas_call x0 -> x2, Pallas kernels: none -> 32.3 us  [the longest x1 28.6 us: kernel_body(): pl.pallas_call(functools.partial(exchange_kernel, dp, tb, cols, rows), na...]
    scatter-add x1 -> x0, other arithmetic: 26.1 us -> none  [accumulate(): return start_total.at[:, target].add(grads.astype(jnp.float32), mode='drop')]
    sub x2 -> x0, other arithmetic: 13.3 us -> none  [the longest x1 13.3 us: body(): table_block - learn_rate * row_grad / jnp.sqrt(new_state)[None, :]]
    unnamed x6 -> x0, local copies, waits for them, and re-layouts: 10.6 us -> none
    all_to_all x1 -> x0, starting transfers between devices: 7.4 us -> none  [body(): lax.all_to_all(gradients, 'table', split_axis=0, concat_axis=1, tiled=True)]
    reduce_sum x1 -> x0, other arithmetic: 5.28 us -> none  [body(): partial_squares = jnp.sum(row_grad * row_grad, axis=0)]
  transfers between devices with their start and end apart: 2 -> 0, of which waited for: 1 -> 0; matrix products, arithmetic and copies ran while one was open for 2% -> 0% of each run, Pallas kernels for 0% -> 0%
where the time goes in v1:
time: 33.1 us; the launch traced here: 32.9 us
  Pallas kernels  32.3 us (98%)
  between operations  0.64 us (2%)
    pallas_call x1, Pallas kernels, kernel_body(): pl.pallas_call(functools.partial(exchange_kernel, dp, tb, cols, rows), na...  28.6 us
    pallas_call x1, Pallas kernels, kernel_body(): pl.pallas_call(functools.partial(update_kernel, width, cols), name='updat...  3.68 us

profile of v1, /device:TPU:0, one launch (start us, length us, event | category | flops | bytes accessed | tf_op | source)
XLA Modules:
  0.0 32.9 jit_solution(17218967866996108780)
XLA Ops:
  0.6 28.6 %exchange.1 = (f32[1024,256]{1,0:T(8,128)}, f32[16,8,128]{2,1,0:T(8,128)}) custom-call(bf16[16,16,128]{2,1,0:T(8,128)(2,1)} %bitcast.7, s32[1,128]{1,0:T(1,128)} %bitcast.8), custom_call_target="tpu_custom_call" | custom-call | tf_op jit(solution)/shard_map/exchange/pallas_call | solution.py:196
  29.3 3.7 %update.1 = (f32[16,16384]{1,0:T(8,128)}, f32[128,128]{1,0:T(8,128)}) custom-call(f32[1024,256]{1,0:T(8,128)} %get-tuple-element.6.acc_ref, f32[128,128]{1,0:T(8,128)} %bitcast.6, f32[128,128]{1,0:T(8,128)} %bitcast.5, f32[16,16384]{1,0:T(8,128)} %table_ref.1), custom_call_target="tpu_custom_call" | custom-call | tf_op jit(solution)/shard_map/update/pallas_call | solution.py:228

commit v2 on v1

v2 whole, which is shorter than its diff:
```python
import functools

import jax
import jax.numpy as jnp
from jax import lax
from jax.experimental import pallas as pl
from jax.experimental.pallas import tpu as pltpu
from jax.sharding import PartitionSpec as P

learn_rate = 0.5
LO = 256
LANES = 128
MESH = pl.DeviceIdType.MESH


def accumulate(grads, ids, first_row, count_rows):
    relative = ids - first_row
    inside = (relative >= 0) & (relative < count_rows)
    target = jnp.where(inside, relative, count_rows)
    start_total = jnp.zeros((grads.shape[0], count_rows), jnp.float32)
    return start_total.at[:, target].add(grads.astype(jnp.float32), mode="drop")


def plain_body(width, gradients, row_ids, table_block, adagrad_state):
    owned = lax.all_to_all(gradients, "table", split_axis=0, concat_axis=1, tiled=True)
    local_rows = table_block.shape[1]
    all_row_ids = lax.all_gather(row_ids, ("dp", "table"), axis=0, tiled=True)
    first_row = lax.axis_index("dp") * local_rows
    row_grad = accumulate(
        lax.all_gather(owned, "dp", axis=1, tiled=True), all_row_ids, first_row, local_rows
    )
    partial_squares = jnp.sum(row_grad * row_grad, axis=0)
    squares = lax.psum(partial_squares, "table")
    new_state = adagrad_state + squares / width
    new_table = table_block - learn_rate * row_grad / jnp.sqrt(new_state)[None, :]
    return (new_table, new_state)


def flip(value, by, size):
    out, bit = 0, 1
    while bit < size:
        out = out + lax.rem(value // bit + by // bit, 2) * bit
        bit *= 2
    return out


def exchange_kernel(
    dp, tb, cols, rows, width,
    g_ref, id_ref, state_ref, table_ref, table_out, state_out,
    acc, got_g, got_i, table, part, red, total, full, state,
    send_g, send_i, send_r, send_a, recv_g, recv_i, recv_r, recv_a, own_sem,
):
    d, t = lax.axis_index("dp"), lax.axis_index("table")
    n = dp * tb
    me = d * tb + t
    his = rows // LO
    lines = rows // tb // LANES
    parts = LO // LANES
    first_row = d * rows

    def device(k):
        side = flip(t, lax.rem(k, 4) + (k // (4 * dp)) * 4, tb)
        return flip(d, lax.rem(k // 4, dp), dp), side

    barrier = pltpu.get_barrier_semaphore()

    @pl.loop(1, n)
    def _(k):
        pl.semaphore_signal(barrier, inc=1, device_id=device(n - k), device_id_type=MESH)

    own = (
        pltpu.make_async_copy(g_ref.at[t], got_g.at[me], own_sem.at[0]),
        pltpu.make_async_copy(id_ref, got_i.at[me], own_sem.at[1]),
        pltpu.make_async_copy(state_ref, state, own_sem.at[2]),
        pltpu.make_async_copy(table_ref, table, own_sem.at[3]),
    )
    for copy in own:
        copy.start()
    acc[...] = jnp.zeros_like(acc)
    pl.semaphore_wait(barrier, n - 1)

    def block_copies(k):
        to = device(k)
        peer = to[0] * tb + to[1]
        return (
            pltpu.make_async_remote_copy(
                src_ref=id_ref, dst_ref=got_i.at[me],
                send_sem=send_i.at[peer], recv_sem=recv_i.at[me],
                device_id=to, device_id_type=MESH,
            ),
            pltpu.make_async_remote_copy(
                src_ref=g_ref.at[to[1]], dst_ref=got_g.at[me],
                send_sem=send_g.at[peer], recv_sem=recv_g.at[me],
                device_id=to, device_id_type=MESH,
            ),
        )

    @pl.loop(1, n)
    def _(k):
        for copy in block_copies(k):
            copy.start()

    def arrived(k):
        there = device(k)
        source = there[0] * tb + there[1]
        pltpu.make_async_copy(id_ref, got_i.at[source], recv_i.at[source]).wait()
        pltpu.make_async_copy(g_ref.at[t], got_g.at[source], recv_g.at[source]).wait()
        return source

    def add(sources):
        ids = jnp.concatenate([got_i[k] for k in sources], axis=1) - first_row
        grads = jnp.concatenate([got_g[k] for k in sources], axis=1)
        span = ids.shape[1]
        low = jnp.broadcast_to(lax.bitwise_and(ids, LO - 1), (LO, span))
        place = lax.broadcasted_iota(jnp.int32, (LO, span), 0)
        one_hot = jnp.where(low == place, 1.0, 0.0).astype(jnp.bfloat16)
        high = jnp.broadcast_to(lax.shift_right_arithmetic(ids, 8), (cols, span))
        high = jnp.clip(high, -1, his).astype(jnp.float32).astype(jnp.bfloat16)
        zero = jnp.zeros_like(grads)
        picked = jnp.concatenate(
            [jnp.where(high == jnp.bfloat16(h), grads, zero) for h in range(his)], axis=0
        )
        acc[...] += lax.dot_general(
            picked, one_hot, (((1,), (1,)), ((), ())), preferred_element_type=jnp.float32
        )

    own[0].wait()
    own[1].wait()
    GROUP = 4
    add([me] + [arrived(k) for k in range(1, GROUP)])

    @pl.loop(1, n // GROUP)
    def _(k):
        add([arrived(GROUP * k + i) for i in range(GROUP)])

    each = his // tb
    for j in range(tb):
        pieces = []
        for h in range(each):
            at = (j * each + h) * cols
            piece = acc[at:at + cols, :]
            sums = jnp.sum(piece * piece, axis=0, keepdims=True)
            for half in range(parts):
                pieces.append(sums[:, half * LANES:(half + 1) * LANES])
        part[j] = jnp.concatenate(pieces, axis=0)

    @pl.loop(1, tb)
    def _(k):
        to = flip(t, tb - k, tb)
        pltpu.make_async_remote_copy(
            src_ref=part.at[to], dst_ref=red.at[t],
            send_sem=send_r.at[to], recv_sem=recv_r.at[t],
            device_id=(d, to), device_id_type=MESH,
        ).start()

    own[2].wait()
    own[3].wait()
    red[t] = part[t]

    @pl.loop(1, tb)
    def _(k):
        source = flip(t, k, tb)
        pltpu.make_async_copy(part.at[t], red.at[source], recv_r.at[source]).wait()

    here = pl.ds(pl.multiple_of(t * lines, lines), lines)
    total[...] = state[here, :] + jnp.sum(red[...], axis=0) / width
    full[t] = total[...]

    @pl.loop(1, tb)
    def _(k):
        to = flip(t, tb - k, tb)
        pltpu.make_async_copy(part.at[to], red.at[t], send_r.at[to]).wait()

    @pl.loop(1, tb)
    def _(k):
        to = flip(t, tb - k, tb)
        pltpu.make_async_remote_copy(
            src_ref=total, dst_ref=full.at[t],
            send_sem=send_a.at[to], recv_sem=recv_a.at[t],
            device_id=(d, to), device_id_type=MESH,
        ).start()

    def update(j):
        fresh = full[j]
        state_out[j] = fresh
        scale = learn_rate / jnp.sqrt(fresh)
        for r in range(lines):
            h, half = r // parts, r % parts
            at = pl.multiple_of((j * each + h) * cols, cols)
            lanes = pl.ds(pl.multiple_of((j * lines + r) * LANES, LANES), LANES)
            step = acc[pl.ds(at, cols), half * LANES:(half + 1) * LANES]
            table_out[:, lanes] = table[:, lanes] - step * scale[r:r + 1, :]

    @pl.loop(1, n)
    def _(k):
        for copy in block_copies(k):
            copy.wait_send()

    update(t)

    @pl.loop(1, tb)
    def _(k):
        source = flip(t, k, tb)
        pltpu.make_async_copy(total, full.at[source], recv_a.at[source]).wait()
        update(source)

    @pl.loop(1, tb)
    def _(k):
        to = flip(t, tb - k, tb)
        pltpu.make_async_copy(total, full.at[t], send_a.at[to]).wait()


def kernel_body(dp, tb, width, gradients, row_ids, table_block, adagrad_state):
    cols, rows = table_block.shape
    count = row_ids.shape[0]
    n = dp * tb
    his = rows // LO
    lines = rows // tb // LANES
    dma = pltpu.SemaphoreType.DMA
    new_table, new_state = pl.pallas_call(
        functools.partial(exchange_kernel, dp, tb, cols, rows, width),
        name="exchange",
        out_shape=(
            pltpu.VMEM((cols, rows), jnp.float32),
            pltpu.VMEM((tb, lines, LANES), jnp.float32),
        ),
        in_specs=[pl.BlockSpec(memory_space=pl.ANY)] * 4,
        out_specs=(pl.BlockSpec(memory_space=pltpu.VMEM),) * 2,
        scratch_shapes=[
            pltpu.VMEM((his * cols, LO), jnp.float32),
            pltpu.VMEM((n, cols, count), jnp.bfloat16),
            pltpu.VMEM((n, 1, count), jnp.int32),
            pltpu.VMEM((cols, rows), jnp.float32),
            pltpu.VMEM((tb, lines, LANES), jnp.float32),
            pltpu.VMEM((tb, lines, LANES), jnp.float32),
            pltpu.VMEM((lines, LANES), jnp.float32),
            pltpu.VMEM((tb, lines, LANES), jnp.float32),
            pltpu.VMEM((rows // LANES, LANES), jnp.float32),
            dma((n,)), dma((n,)), dma((tb,)), dma((tb,)),
            dma((n,)), dma((n,)), dma((tb,)), dma((tb,)),
            dma((4,)),
        ],
        compiler_params=pltpu.CompilerParams(collective_id=0, has_side_effects=True),
    )(
        gradients.reshape(tb, cols, count),
        row_ids.reshape(1, count),
        adagrad_state.reshape(rows // LANES, LANES),
        table_block,
    )
    return (new_table, new_state.reshape(rows))


def body(dp, tb, gradients, row_ids, table_block, adagrad_state):
    width = gradients.shape[0]
    cols, rows = table_block.shape
    fits = (
        cols % 16 == 0
        and rows % (tb * 8 * LANES) == 0
        and rows % (4 * LO * 4) == 0
        and dp & (dp - 1) == 0
        and tb & (tb - 1) == 0
        and tb % 4 == 0
        and rows // LO <= 256
        and row_ids.shape[0] == LANES
    )
    args = (gradients, row_ids, table_block, adagrad_state)
    if fits:
        return kernel_body(dp, tb, width, *args)
    return plain_body(width, *args)


def solution(mesh):
    in_specs = (P(None, ("dp", "table")), P(("dp", "table")), P("table", "dp"), P("dp"))
    out_specs = (P("table", "dp"), P("dp"))
    run = functools.partial(body, mesh.shape["dp"], mesh.shape["table"])
    return jax.shard_map(run, mesh=mesh, in_specs=in_specs, out_specs=out_specs, check_vma=False)
```

time: 33.1 us -> 28.2 us (0.85)
  Pallas kernels: 32.3 us -> 25.8 us
  local copies, waits for them, and re-layouts: 0 us -> 1.61 us
    pallas_call x2 -> x1, Pallas kernels: 32.3 us -> 25.8 us  [kernel_body(): pl.pallas_call(functools.partial(exchange_kernel, dp, tb, cols, rows, wid...]
    unnamed x0 -> x2, local copies, waits for them, and re-layouts: none -> 1.61 us
where the time goes in v2:
time: 28.2 us; the launch traced here: 28.1 us
  Pallas kernels  25.8 us (91%)
  local copies, waits for them, and re-layouts  1.61 us (6%)
  between operations  0.64 us (2%)
    pallas_call x1, Pallas kernels, kernel_body(): pl.pallas_call(functools.partial(exchange_kernel, dp, tb, cols, rows, wid...  25.8 us
    unnamed x2, local copies, waits for them, and re-layouts  1.61 us

profile of v2, /device:TPU:0, one launch (start us, length us, event | category | flops | bytes accessed | tf_op | source)
XLA Modules:
  0.0 28.1 jit_solution(17083477167339699988)
XLA Ops:
  0.6 25.8 %exchange.1 = (f32[16,16384]{1,0:T(8,128)S(1)}, f32[16,8,128]{2,1,0:T(8,128)S(1)}) custom-call(bf16[16,16,128]{2,1,0:T(8,128)(2,1)} %bitcast.5, s32[1,128]{1,0:T(1,128)} %bitcast.7, f32[128,128]{1,0:T(8,128)} %bitcast.6, f32[16,16384]{1,0:T(8,128)} %table_ref.1), custom_call_target="tpu_custom_call" | custom-call | tf_op jit(solution)/shard_map/exchange/pallas_call | solution.py:220
  26.4 1.0 %copy.8 = f32[16,16384]{1,0:T(8,128)} copy(f32[16,16384]{1,0:T(8,128)S(1)} %get-tuple-element.6) | data formatting | bytes 2097152
  27.4 0.6 %copy.9 = f32[16384]{0:T(1024)} copy(f32[16384]{0:T(1024)S(1)} %bitcast.4) | data formatting | bytes 131072

commit v3 on v2

--- a/solution.py
+++ b/solution.py
@@ -10,6 +10,7 @@
 learn_rate = 0.5
 LO = 256
 LANES = 128
+GROUP = 4
 MESH = pl.DeviceIdType.MESH
 
 
@@ -36,12 +37,13 @@
     return (new_table, new_state)
 
 
-def flip(value, by, size):
-    out, bit = 0, 1
+def flips(value, size):
+    table, bit = [value], 1
     while bit < size:
-        out = out + lax.rem(value // bit + by // bit, 2) * bit
+        change = bit - 2 * bit * lax.rem(value // bit, 2)
+        table = table + [old + change for old in table]
         bit *= 2
-    return out
+    return table
 
 
 def exchange_kernel(
@@ -54,19 +56,21 @@
     n = dp * tb
     me = d * tb + t
     his = rows // LO
-    lines = rows // tb // LANES
+    teams = tb // 2
+    base = tb // 4
+    lines = rows // teams // LANES
     parts = LO // LANES
+    each = his // teams
     first_row = d * rows
+    ts, ds = flips(t, tb), flips(d, dp)
+    reducer = jnp.logical_and(t >= base, t < base + teams)
 
     def device(k):
-        side = flip(t, lax.rem(k, 4) + (k // (4 * dp)) * 4, tb)
-        return flip(d, lax.rem(k // 4, dp), dp), side
+        return ds[k // 4 % dp], ts[k % 4 + k // (4 * dp) * 4]
 
     barrier = pltpu.get_barrier_semaphore()
-
-    @pl.loop(1, n)
-    def _(k):
-        pl.semaphore_signal(barrier, inc=1, device_id=device(n - k), device_id_type=MESH)
+    for k in reversed(range(1, n)):
+        pl.semaphore_signal(barrier, inc=1, device_id=device(k), device_id_type=MESH)
 
     own = (
         pltpu.make_async_copy(g_ref.at[t], got_g.at[me], own_sem.at[0]),
@@ -81,30 +85,28 @@
 
     def block_copies(k):
         to = device(k)
-        peer = to[0] * tb + to[1]
         return (
             pltpu.make_async_remote_copy(
                 src_ref=id_ref, dst_ref=got_i.at[me],
-                send_sem=send_i.at[peer], recv_sem=recv_i.at[me],
+                send_sem=send_i.at[k], recv_sem=recv_i.at[k],
                 device_id=to, device_id_type=MESH,
             ),
             pltpu.make_async_remote_copy(
                 src_ref=g_ref.at[to[1]], dst_ref=got_g.at[me],
-                send_sem=send_g.at[peer], recv_sem=recv_g.at[me],
+                send_sem=send_g.at[k], recv_sem=recv_g.at[k],
                 device_id=to, device_id_type=MESH,
             ),
         )
 
-    @pl.loop(1, n)
-    def _(k):
+    for k in range(1, n):
         for copy in block_copies(k):
             copy.start()
 
     def arrived(k):
         there = device(k)
         source = there[0] * tb + there[1]
-        pltpu.make_async_copy(id_ref, got_i.at[source], recv_i.at[source]).wait()
-        pltpu.make_async_copy(g_ref.at[t], got_g.at[source], recv_g.at[source]).wait()
+        pltpu.make_async_copy(id_ref, got_i.at[source], recv_i.at[k]).wait()
+        pltpu.make_async_copy(g_ref.at[t], got_g.at[source], recv_g.at[k]).wait()
         return source
 
     def add(sources):
@@ -126,15 +128,11 @@
 
     own[0].wait()
     own[1].wait()
-    GROUP = 4
     add([me] + [arrived(k) for k in range(1, GROUP)])
-
-    @pl.loop(1, n // GROUP)
-    def _(k):
-        add([arrived(GROUP * k + i) for i in range(GROUP)])
-
-    each = his // tb
-    for j in range(tb):
+    for first in range(GROUP, n, GROUP):
+        add([arrived(k) for k in range(first, first + GROUP)])
+
+    for j in range(teams):
         pieces = []
         for h in range(each):
             at = (j * each + h) * cols
@@ -144,41 +142,45 @@
                 pieces.append(sums[:, half * LANES:(half + 1) * LANES])
         part[j] = jnp.concatenate(pieces, axis=0)
 
-    @pl.loop(1, tb)
-    def _(k):
-        to = flip(t, tb - k, tb)
-        pltpu.make_async_remote_copy(
-            src_ref=part.at[to], dst_ref=red.at[t],
-            send_sem=send_r.at[to], recv_sem=recv_r.at[t],
-            device_id=(d, to), device_id_type=MESH,
-        ).start()
+    def part_copy(k):
+        team = lax.rem(t + (tb - base + k), teams)
+        return pltpu.make_async_remote_copy(
+            src_ref=part.at[team], dst_ref=red.at[t],
+            send_sem=send_r.at[k], recv_sem=recv_r.at[t],
+            device_id=(d, team + base), device_id_type=MESH,
+        )
+
+    for k in reversed(range(1, teams)):
+        part_copy(k).start()
+
+    @pl.when(jnp.logical_not(reducer))
+    def _():
+        part_copy(0).start()
 
     own[2].wait()
     own[3].wait()
-    red[t] = part[t]
-
-    @pl.loop(1, tb)
-    def _(k):
-        source = flip(t, k, tb)
-        pltpu.make_async_copy(part.at[t], red.at[source], recv_r.at[source]).wait()
-
-    here = pl.ds(pl.multiple_of(t * lines, lines), lines)
-    total[...] = state[here, :] + jnp.sum(red[...], axis=0) / width
-    full[t] = total[...]
-
-    @pl.loop(1, tb)
-    def _(k):
-        to = flip(t, tb - k, tb)
-        pltpu.make_async_copy(part.at[to], red.at[t], send_r.at[to]).wait()
-
-    @pl.loop(1, tb)
-    def _(k):
-        to = flip(t, tb - k, tb)
-        pltpu.make_async_remote_copy(
-            src_ref=total, dst_ref=full.at[t],
-            send_sem=send_a.at[to], recv_sem=recv_a.at[t],
-            device_id=(d, to), device_id_type=MESH,
-        ).start()
+
+    def total_copy(k):
+        return pltpu.make_async_remote_copy(
+            src_ref=total, dst_ref=full.at[t - base],
+            send_sem=send_a.at[k], recv_sem=recv_a.at[t - base],
+            device_id=(d, ts[k]), device_id_type=MESH,
+        )
+
+    @pl.when(reducer)
+    def _():
+        mine = t - base
+        red[t] = part[mine]
+        for k in range(1, tb):
+            pltpu.make_async_copy(part.at[0], red.at[ts[k]], recv_r.at[ts[k]]).wait()
+        here = pl.ds(pl.multiple_of(mine * lines, lines), lines)
+        fresh = state[here, :] + jnp.sum(red[...], axis=0) / width
+        total[...] = fresh
+        full[mine] = fresh
+        for k in range(1, teams):
+            part_copy(k).wait_send()
+        for k in reversed(range(1, tb)):
+            total_copy(k).start()
 
     def update(j):
         fresh = full[j]
@@ -191,23 +193,33 @@
             step = acc[pl.ds(at, cols), half * LANES:(half + 1) * LANES]
             table_out[:, lanes] = table[:, lanes] - step * scale[r:r + 1, :]
 
-    @pl.loop(1, n)
-    def _(k):
+    for k in range(1, n):
         for copy in block_copies(k):
             copy.wait_send()
 
-    update(t)
-
-    @pl.loop(1, tb)
+    def receive(k):
+        team = lax.rem(t + (tb - base + k), teams)
+        pltpu.make_async_copy(total, full.at[team], recv_a.at[team]).wait()
+        update(team)
+
+    @pl.when(reducer)
+    def _():
+        update(t - base)
+
+    @pl.when(jnp.logical_not(reducer))
+    def _():
+        receive(0)
+        for k in range(teams):
+            part_copy(k).wait_send()
+
+    @pl.loop(1, teams)
     def _(k):
-        source = flip(t, k, tb)
-        pltpu.make_async_copy(total, full.at[source], recv_a.at[source]).wait()
-        update(source)
-
-    @pl.loop(1, tb)
-    def _(k):
-        to = flip(t, tb - k, tb)
-        pltpu.make_async_copy(total, full.at[t], send_a.at[to]).wait()
+        receive(k)
+
+    @pl.when(reducer)
+    def _():
+        for k in range(1, tb):
+            total_copy(k).wait_send()
 
 
 def kernel_body(dp, tb, width, gradients, row_ids, table_block, adagrad_state):
@@ -215,14 +227,15 @@
     count = row_ids.shape[0]
     n = dp * tb
     his = rows // LO
-    lines = rows // tb // LANES
+    teams = tb // 2
+    lines = rows // teams // LANES
     dma = pltpu.SemaphoreType.DMA
     new_table, new_state = pl.pallas_call(
         functools.partial(exchange_kernel, dp, tb, cols, rows, width),
         name="exchange",
         out_shape=(
             pltpu.VMEM((cols, rows), jnp.float32),
-            pltpu.VMEM((tb, lines, LANES), jnp.float32),
+            pltpu.VMEM((teams, lines, LANES), jnp.float32),
         ),
         in_specs=[pl.BlockSpec(memory_space=pl.ANY)] * 4,
         out_specs=(pl.BlockSpec(memory_space=pltpu.VMEM),) * 2,
@@ -231,13 +244,13 @@
             pltpu.VMEM((n, cols, count), jnp.bfloat16),
             pltpu.VMEM((n, 1, count), jnp.int32),
             pltpu.VMEM((cols, rows), jnp.float32),
-            pltpu.VMEM((tb, lines, LANES), jnp.float32),
+            pltpu.VMEM((teams, lines, LANES), jnp.float32),
             pltpu.VMEM((tb, lines, LANES), jnp.float32),
             pltpu.VMEM((lines, LANES), jnp.float32),
-            pltpu.VMEM((tb, lines, LANES), jnp.float32),
+            pltpu.VMEM((teams, lines, LANES), jnp.float32),
             pltpu.VMEM((rows // LANES, LANES), jnp.float32),
-            dma((n,)), dma((n,)), dma((tb,)), dma((tb,)),
-            dma((n,)), dma((n,)), dma((tb,)), dma((tb,)),
+            dma((n,)), dma((n,)), dma((teams,)), dma((tb,)),
+            dma((n,)), dma((n,)), dma((tb,)), dma((teams,)),
             dma((4,)),
         ],
         compiler_params=pltpu.CompilerParams(collective_id=0, has_side_effects=True),

time: 28.2 us -> 27.3 us (0.968)
  Pallas kernels: 25.8 us -> 24.9 us
    pallas_call x1, Pallas kernels: 25.8 us -> 24.9 us  [kernel_body(): pl.pallas_call(functools.partial(exchange_kernel, dp, tb, cols, rows, wid...]
where the time goes in v3:
time: 27.3 us; the launch traced here: 27.2 us
  Pallas kernels  24.9 us (91%)
  local copies, waits for them, and re-layouts  1.61 us (6%)
  between operations  0.64 us (2%)
    pallas_call x1, Pallas kernels, kernel_body(): pl.pallas_call(functools.partial(exchange_kernel, dp, tb, cols, rows, wid...  24.9 us
    unnamed x2, local copies, waits for them, and re-layouts  1.61 us

profile of v3, /device:TPU:0, one launch (start us, length us, event | category | flops | bytes accessed | tf_op | source)
XLA Modules:
  0.0 27.2 jit_solution(1040834788648556993)
XLA Ops:
  0.6 24.9 %exchange.1 = (f32[16,16384]{1,0:T(8,128)S(1)}, f32[8,16,128]{2,1,0:T(8,128)S(1)}) custom-call(bf16[16,16,128]{2,1,0:T(8,128)(2,1)} %bitcast.5, s32[1,128]{1,0:T(1,128)} %bitcast.7, f32[128,128]{1,0:T(8,128)} %bitcast.6, f32[16,16384]{1,0:T(8,128)} %table_ref.1), custom_call_target="tpu_custom_call" | custom-call | tf_op jit(solution)/shard_map/exchange/pallas_call | solution.py:233
  25.5 1.0 %copy.8 = f32[16,16384]{1,0:T(8,128)} copy(f32[16,16384]{1,0:T(8,128)S(1)} %get-tuple-element.6) | data formatting | bytes 2097152
  26.5 0.6 %copy.9 = f32[16384]{0:T(1024)} copy(f32[16384]{0:T(1024)S(1)} %bitcast.4) | data formatting | bytes 131072

commit v4 on v3

--- a/solution.py
+++ b/solution.py
@@ -11,6 +11,7 @@
 LO = 256
 LANES = 128
 GROUP = 4
+PIECES = 4
 MESH = pl.DeviceIdType.MESH
 
 
@@ -49,7 +50,7 @@
 def exchange_kernel(
     dp, tb, cols, rows, width,
     g_ref, id_ref, state_ref, table_ref, table_out, state_out,
-    acc, got_g, got_i, table, part, red, total, full, state,
+    acc, got_g, got_i, near_g, near_i, table, part, red, total, full, state,
     send_g, send_i, send_r, send_a, recv_g, recv_i, recv_r, recv_a, own_sem,
 ):
     d, t = lax.axis_index("dp"), lax.axis_index("table")
@@ -73,26 +74,30 @@
         pl.semaphore_signal(barrier, inc=1, device_id=device(k), device_id_type=MESH)
 
     own = (
-        pltpu.make_async_copy(g_ref.at[t], got_g.at[me], own_sem.at[0]),
-        pltpu.make_async_copy(id_ref, got_i.at[me], own_sem.at[1]),
+        pltpu.make_async_copy(g_ref, near_g, own_sem.at[0]),
+        pltpu.make_async_copy(id_ref, near_i, own_sem.at[1]),
         pltpu.make_async_copy(state_ref, state, own_sem.at[2]),
         pltpu.make_async_copy(table_ref, table, own_sem.at[3]),
     )
     for copy in own:
         copy.start()
     acc[...] = jnp.zeros_like(acc)
+    own[0].wait()
+    own[1].wait()
+    got_g[me] = near_g[t]
+    got_i[me] = near_i[...]
     pl.semaphore_wait(barrier, n - 1)
 
     def block_copies(k):
         to = device(k)
         return (
             pltpu.make_async_remote_copy(
-                src_ref=id_ref, dst_ref=got_i.at[me],
+                src_ref=near_i, dst_ref=got_i.at[me],
                 send_sem=send_i.at[k], recv_sem=recv_i.at[k],
                 device_id=to, device_id_type=MESH,
             ),
             pltpu.make_async_remote_copy(
-                src_ref=g_ref.at[to[1]], dst_ref=got_g.at[me],
+                src_ref=near_g.at[to[1]], dst_ref=got_g.at[me],
                 send_sem=send_g.at[k], recv_sem=recv_g.at[k],
                 device_id=to, device_id_type=MESH,
             ),
@@ -105,8 +110,8 @@
     def arrived(k):
         there = device(k)
         source = there[0] * tb + there[1]
-        pltpu.make_async_copy(id_ref, got_i.at[source], recv_i.at[k]).wait()
-        pltpu.make_async_copy(g_ref.at[t], got_g.at[source], recv_g.at[k]).wait()
+        pltpu.make_async_copy(near_i, got_i.at[source], recv_i.at[k]).wait()
+        pltpu.make_async_copy(near_g.at[t], got_g.at[source], recv_g.at[k]).wait()
         return source
 
     def add(sources):
@@ -126,8 +131,6 @@
             picked, one_hot, (((1,), (1,)), ((), ())), preferred_element_type=jnp.float32
         )
 
-    own[0].wait()
-    own[1].wait()
     add([me] + [arrived(k) for k in range(1, GROUP)])
     for first in range(GROUP, n, GROUP):
         add([arrived(k) for k in range(first, first + GROUP)])
@@ -220,6 +223,22 @@
     def _():
         for k in range(1, tb):
             total_copy(k).wait_send()
+
+
+def finish_kernel(table_ref, state_ref, table_out, state_out, sems):
+    rows = table_ref.shape[1]
+    size = rows // PIECES
+    copies = [
+        pltpu.make_async_copy(
+            table_ref.at[:, pl.ds(p * size, size)], table_out.at[:, pl.ds(p * size, size)], sems.at[p]
+        )
+        for p in range(PIECES)
+    ]
+    copies.append(pltpu.make_async_copy(state_ref, state_out, sems.at[PIECES]))
+    for copy in copies:
+        copy.start()
+    for copy in copies:
+        copy.wait()
 
 
 def kernel_body(dp, tb, width, gradients, row_ids, table_block, adagrad_state):
@@ -243,6 +262,8 @@
             pltpu.VMEM((his * cols, LO), jnp.float32),
             pltpu.VMEM((n, cols, count), jnp.bfloat16),
             pltpu.VMEM((n, 1, count), jnp.int32),
+            pltpu.VMEM((tb, cols, count), jnp.bfloat16),
+            pltpu.VMEM((1, count), jnp.int32),
             pltpu.VMEM((cols, rows), jnp.float32),
             pltpu.VMEM((teams, lines, LANES), jnp.float32),
             pltpu.VMEM((tb, lines, LANES), jnp.float32),
@@ -260,6 +281,20 @@
         adagrad_state.reshape(rows // LANES, LANES),
         table_block,
     )
+    new_table, new_state = pl.pallas_call(
+        finish_kernel,
+        name="finish",
+        out_shape=(
+            jax.ShapeDtypeStruct((cols, rows), jnp.float32),
+            jax.ShapeDtypeStruct((teams, lines, LANES), jnp.float32),
+        ),
+        in_specs=[pl.BlockSpec(memory_space=pltpu.VMEM)] * 2,
+        out_specs=(pl.BlockSpec(memory_space=pl.ANY),) * 2,
+        scratch_shapes=[dma((PIECES + 1,))],
+    )(
+        pltpu.with_memory_space_constraint(new_table, pltpu.VMEM),
+        pltpu.with_memory_space_constraint(new_state, pltpu.VMEM),
+    )
     return (new_table, new_state.reshape(rows))
 
 

time: 27.3 us -> 26.5 us (0.971)
  local copies, waits for them, and re-layouts: 1.61 us -> 0 us
  Pallas kernels: 24.9 us -> 25.8 us
    unnamed x2 -> x0, local copies, waits for them, and re-layouts: 1.61 us -> none
    pallas_call x0 -> x1, Pallas kernels: none -> 1.02 us  [kernel_body(): pl.pallas_call(finish_kernel, name='finish', out_shape=(jax.ShapeDtypeStr...]
where the time goes in v4:
time: 26.5 us; the launch traced here: 26.4 us
  Pallas kernels  25.8 us (97%)
  between operations  0.64 us (2%)
    pallas_call x1, Pallas kernels, kernel_body(): pl.pallas_call(functools.partial(exchange_kernel, dp, tb, cols, rows, wid...  24.7 us
    pallas_call x1, Pallas kernels, kernel_body(): pl.pallas_call(finish_kernel, name='finish', out_shape=(jax.ShapeDtypeStr...  1.02 us

profile of v4, /device:TPU:0, one launch (start us, length us, event | category | flops | bytes accessed | tf_op | source)
XLA Modules:
  0.0 26.4 jit_solution(16285929314245792475)
XLA Ops:
  0.6 24.7 %exchange.1 = (f32[16,16384]{1,0:T(8,128)S(1)}, f32[8,16,128]{2,1,0:T(8,128)S(1)}) custom-call(bf16[16,16,128]{2,1,0:T(8,128)(2,1)} %bitcast.4, s32[1,128]{1,0:T(1,128)} %bitcast.6, f32[128,128]{1,0:T(8,128)} %bitcast.5, f32[16,16384]{1,0:T(8,128)} %table_ref.1), custom_call_target="tpu_custom_call" | custom-call | tf_op jit(solution)/shard_map/exchange/pallas_call | solution.py:252
  25.4 1.0 %finish.1 = (f32[16,16384]{1,0:T(8,128)}, f32[8,16,128]{2,1,0:T(8,128)}) custom-call(f32[16,16384]{1,0:T(8,128)S(1)} %get-tuple-element.6.table_ref, f32[8,16,128]{2,1,0:T(8,128)S(1)} %get-tuple-element.7.state_ref), custom_call_target="tpu_custom_call" | custom-call | tf_op jit(solution)/shard_map/finish/pallas_call | solution.py:284

commit v5 on v4

--- a/solution.py
+++ b/solution.py
@@ -57,8 +57,8 @@
     n = dp * tb
     me = d * tb + t
     his = rows // LO
-    teams = tb // 2
-    base = tb // 4
+    teams = tb
+    base = 0
     lines = rows // teams // LANES
     parts = LO // LANES
     each = his // teams
@@ -146,7 +146,7 @@
         part[j] = jnp.concatenate(pieces, axis=0)
 
     def part_copy(k):
-        team = lax.rem(t + (tb - base + k), teams)
+        team = ts[k]
         return pltpu.make_async_remote_copy(
             src_ref=part.at[team], dst_ref=red.at[t],
             send_sem=send_r.at[k], recv_sem=recv_r.at[t],
@@ -155,10 +155,6 @@
 
     for k in reversed(range(1, teams)):
         part_copy(k).start()
-
-    @pl.when(jnp.logical_not(reducer))
-    def _():
-        part_copy(0).start()
 
     own[2].wait()
     own[3].wait()
@@ -209,12 +205,6 @@
     def _():
         update(t - base)
 
-    @pl.when(jnp.logical_not(reducer))
-    def _():
-        receive(0)
-        for k in range(teams):
-            part_copy(k).wait_send()
-
     @pl.loop(1, teams)
     def _(k):
         receive(k)
@@ -246,7 +236,7 @@
     count = row_ids.shape[0]
     n = dp * tb
     his = rows // LO
-    teams = tb // 2
+    teams = tb
     lines = rows // teams // LANES
     dma = pltpu.SemaphoreType.DMA
     new_table, new_state = pl.pallas_call(

time: 26.5 us -> 26.3 us (level)
  Pallas kernels: 25.8 us -> 25.5 us
where the time goes in v5:
time: 26.3 us; the launch traced here: 26.1 us
  Pallas kernels  25.5 us (97%)
  between operations  0.64 us (2%)
    pallas_call x1, Pallas kernels, kernel_body(): pl.pallas_call(functools.partial(exchange_kernel, dp, tb, cols, rows, wid...  24.5 us
    pallas_call x1, Pallas kernels, kernel_body(): pl.pallas_call(finish_kernel, name='finish', out_shape=(jax.ShapeDtypeStr...  1.02 us

profile of v5, /device:TPU:0, one launch (start us, length us, event | category | flops | bytes accessed | tf_op | source)
XLA Modules:
  0.0 26.1 jit_solution(11499523924378066023)
XLA Ops:
  0.6 24.5 %exchange.1 = (f32[16,16384]{1,0:T(8,128)S(1)}, f32[16,8,128]{2,1,0:T(8,128)S(1)}) custom-call(bf16[16,16,128]{2,1,0:T(8,128)(2,1)} %bitcast.4, s32[1,128]{1,0:T(1,128)} %bitcast.6, f32[128,128]{1,0:T(8,128)} %bitcast.5, f32[16,16384]{1,0:T(8,128)} %table_ref.1), custom_call_target="tpu_custom_call" | custom-call | tf_op jit(solution)/shard_map/exchange/pallas_call | solution.py:242
  25.1 1.0 %finish.1 = (f32[16,16384]{1,0:T(8,128)}, f32[16,8,128]{2,1,0:T(8,128)}) custom-call(f32[16,16384]{1,0:T(8,128)S(1)} %get-tuple-element.6.table_ref, f32[16,8,128]{2,1,0:T(8,128)S(1)} %get-tuple-element.7.state_ref), custom_call_target="tpu_custom_call" | custom-call | tf_op jit(solution)/shard_map/finish/pallas_call | solution.py:274
